TPU v7x, 256 devices: a whole 4x4x8 slice. The times are simulated.
256 devices in a mesh: section: 4 (over y), ctx: 16 (over z, x_hi), tp: 4 (over x_lo, core).
Axes of the slice: x: 4 (x_hi: 2, x_lo: 2; x = x_hi * 2 + x_lo), y: 4, z: 8, core: 2. Of those that a mesh axis runs over, the one named last changes fastest.
Arguments:
- hidden_in: bfloat16 [4, 2048, 4096], P('section', 'ctx', 'tp'), may hold values from -16 to 16
- fresh_in: bfloat16 [3, 2048, 4096], P(None, 'ctx', 'tp'), may hold values from -16 to 16
- block_table: int32 [32], replicated, may hold values from 0 to 31, as said below
- norm_gain: float32 [4, 4096], P('section'), may hold values from 0.1 to 1.9
- w_query: bfloat16 [4, 4096, 4096], P('section', 'ctx', 'tp'), may hold values from -3.125 to 3.125
- w_key: bfloat16 [4, 4096, 512], P('section', 'ctx', 'tp'), may hold values from -0.09375 to 0.09375
- w_value: bfloat16 [4, 4096, 512], P('section', 'ctx', 'tp'), may hold values from -0.09375 to 0.09375
- w_out: bfloat16 [4, 4096, 4096], P('section', 'ctx', 'tp'), may hold values from -0.09375 to 0.09375
Outputs:
- layer_outputs: bfloat16 [4, 4, 2048, 4096], P(None, 'section', 'ctx', 'tp')
Inputs may be any that keep to these rules, and one draw needn't show every extreme that they name: `block_table`: slots 2i and 2i + 1 hold blocks p and 31 - p for some p, in either order; every block appears once.
All inputs are finite; a program needn't handle non-finite values.
Results may differ from a plain program's by a relative error of at most 0.03.
Values may be sent and summed in bfloat16 or wider, within the bound.
No kernel may reach another device: no remote copies, remote signals or barrier semaphores. Data moves between devices by JAX's collectives and lax.ppermute only.
A program may use at most 128 MiB of HBM per device.

v0:
```python
import jax
import jax.numpy as jnp
from jax import lax
from jax.sharding import PartitionSpec as P

HEAD_DIM = 128
BLOCK = 64
EPS = 1e-05
ROPE_BASE = 500000.0
NEGATIVE = -1e30


def shifted(x, axis, by):
    count = lax.axis_size(axis)
    pairs = [(i, i + by) for i in range(count) if 0 <= i + by < count]
    return lax.ppermute(x, axis, pairs)


def rotate(vectors, cosine_table, sine_table):
    half_width = vectors.shape[-1] // 2
    first_half = vectors[..., :half_width]
    second_half = vectors[..., half_width:]
    return jnp.concatenate(
        [
            first_half * cosine_table - second_half * sine_table,
            second_half * cosine_table + first_half * sine_table,
        ],
        axis=-1,
    )


def angle_tables(positions):
    half_width = HEAD_DIM // 2
    frequency = ROPE_BASE ** (-(jnp.arange(half_width, dtype=jnp.float32) * 2.0) / HEAD_DIM)
    angles = positions.astype(jnp.float32)[:, None] * frequency[None, :]
    return (jnp.cos(angles), jnp.sin(angles))


def block_positions(block_table, first_row, row_count):
    row_ids = first_row + jnp.arange(row_count, dtype=jnp.int32)
    slot_ids = row_ids // BLOCK
    matches = slot_ids[:, None] == jnp.arange(block_table.shape[0], dtype=jnp.int32)[None, :]
    owners = jnp.sum(jnp.where(matches, block_table[None, :], 0), axis=1)
    return owners * BLOCK + row_ids % BLOCK


def on_device(hidden_in, fresh_in, block_table, norm_gain, w_query, w_key, w_value, w_out):
    row_count = hidden_in.shape[1]
    sections = lax.axis_size("section")
    query_weights, key_weights, value_weights, output_weights = (
        lax.all_gather(w_query[0], "ctx", axis=0, tiled=True),
        lax.all_gather(w_key[0], "ctx", axis=0, tiled=True),
        lax.all_gather(w_value[0], "ctx", axis=0, tiled=True),
        lax.all_gather(w_out[0], "ctx", axis=0, tiled=True),
    )
    gain_row = norm_gain[0]
    positions = block_positions(block_table, lax.axis_index("ctx") * row_count, row_count)
    cosine_table, sine_table = angle_tables(positions)
    cosine_table = cosine_table[:, None, :]
    sine_table = sine_table[:, None, :]
    query_heads = query_weights.shape[1] // HEAD_DIM
    kv_local = key_weights.shape[1] // HEAD_DIM
    group_size = query_heads // kv_local
    score_scale = HEAD_DIM ** (-0.5)
    first_section = lax.axis_index("section") == 0
    produced = []
    current = hidden_in[0]
    for step_index in range(sections):
        full_rows = lax.all_gather(current, "tp", axis=1, tiled=True)
        widened = full_rows.astype(jnp.float32)
        normed = (
            widened
            * lax.rsqrt(jnp.mean(widened * widened, axis=-1, keepdims=True) + EPS)
            * gain_row
        ).astype(jnp.bfloat16)
        queries = jnp.dot(normed, query_weights, preferred_element_type=jnp.float32).reshape(
            row_count, query_heads, HEAD_DIM
        )
        queries = (
            rotate(queries, cosine_table, sine_table)
            .astype(jnp.bfloat16)
            .reshape(row_count, kv_local, group_size, HEAD_DIM)
        )
        key_vecs = jnp.dot(normed, key_weights, preferred_element_type=jnp.float32).reshape(
            row_count, kv_local, HEAD_DIM
        )
        key_vecs = (
            rotate(key_vecs, cosine_table, sine_table)
            .astype(jnp.bfloat16)
            .reshape(row_count, kv_local * HEAD_DIM)
        )
        values = jnp.dot(normed, value_weights, preferred_element_type=jnp.float32).astype(
            jnp.bfloat16
        )
        key_piece = lax.all_gather(key_vecs, "ctx", axis=0, tiled=True)
        value_piece = lax.all_gather(values, "ctx", axis=0, tiled=True)
        key_count = key_piece.shape[0]
        key_positions = block_positions(block_table, jnp.int32(0), key_count)
        scores = (
            jnp.einsum(
                "rkgd,nkd->kgrn",
                queries,
                key_piece.reshape(key_count, kv_local, HEAD_DIM),
                preferred_element_type=jnp.float32,
            )
            * score_scale
        )
        allowed = key_positions[None, None, None, :] <= positions[None, None, :, None]
        largest = jnp.full((kv_local, group_size, row_count), NEGATIVE, jnp.float32)
        new_largest = jnp.maximum(largest, jnp.max(jnp.where(allowed, scores, NEGATIVE), axis=-1))
        weights = jnp.where(allowed, jnp.exp(scores - new_largest[..., None]), 0.0)
        weight_sum = jnp.sum(weights, axis=-1)
        mixed = jnp.einsum(
            "kgrn,nkd->kgrd",
            weights.astype(jnp.bfloat16),
            value_piece.reshape(key_count, kv_local, HEAD_DIM),
            preferred_element_type=jnp.float32,
        )
        largest, weight_sum, accumulated = (new_largest, weight_sum, mixed)
        attended = (accumulated / weight_sum[..., None]).astype(jnp.bfloat16)
        attended = attended.transpose(2, 0, 1, 3).reshape(row_count, query_heads * HEAD_DIM)
        summed = lax.psum_scatter(
            lax.dot_general(
                attended,
                output_weights,
                (((1,), (1,)), ((), ())),
                preferred_element_type=jnp.float32,
            ).astype(jnp.bfloat16),
            "tp",
            scatter_dimension=1,
            tiled=True,
        ).astype(jnp.float32)
        result = (current.astype(jnp.float32) + summed).astype(jnp.bfloat16)
        produced.append(result)
        if step_index + 1 < sections:
            moved = shifted(result, "section", 1)
            current = jnp.where(first_section, fresh_in[step_index], moved)
    return jnp.stack(produced)[:, None]


def solution(mesh):
    in_specs = (
        P("section", "ctx", "tp"),
        P(None, "ctx", "tp"),
        P(),
        P("section", None),
        P("section", "ctx", "tp"),
        P("section", "ctx", "tp"),
        P("section", "ctx", "tp"),
        P("section", "ctx", "tp"),
    )
    out_specs = P(None, "section", "ctx", "tp")
    return jax.shard_map(
        on_device, mesh=mesh, in_specs=in_specs, out_specs=out_specs, check_vma=False
    )
```

profile of v0, /device:TPU:1, one launch (start us, length us, event | category | flops | bytes accessed | tf_op | source)
XLA Modules:
  0.0 1003.0 jit_solution(7136594776463280632)
XLA Ops:
  12.2 24.3 %all-gather.20.cloned.1.call-done = bf16[1,128,4096]{2,1,0:T(8,128)(2,1)} async-done(((bf16[1,128,1024]{2,1,0:T(8,128)(2,1)}), bf16[1,128,4096]{2,1,0:T(8,128)(2,1)}) %all-gather.20.cloned.1.call-update) | async-done | bytes 1048592 | tf_op jit(solution)/shard_map/all_gather | solution.py:69
  38.1 75.9 %all-gather.22.cloned.1.call-done = bf16[1,4096,128]{2,1,0:T(8,128)(2,1)} async-done(((bf16[1,256,128]{2,1,0:T(8,128)(2,1)}), bf16[1,4096,128]{2,1,0:T(8,128)(2,1)}) %all-gather.22.cloned.1.call-update) | async-done | bytes 1048592 | tf_op jit(solution)/shard_map/all_gather | solution.py:52
  114.0 2.2 convolution_bitcast_fusion.3
  116.4 33.2 %all_gather.50 = bf16[2048,128]{0,1:T(8,128)(2,1)S(1)} all-gather(bf16[128,128]{0,1:T(8,128)(2,1)S(1)} %pad_maximum_fusion), channel_id=1, replica_groups=mesh['section'=4,'ctx'=16,'tp'=4] {'ctx'}, dimensions={0}, use_global_device_ids=true | all-gather | bytes 557056 | tf_op jit(solution)/shard_map/all_gather | solution.py:95
  149.5 42.2 %all-gather.26.cloned.1.call-done = bf16[1,4096,128]{2,1,0:T(8,128)(2,1)} async-done(((bf16[1,256,128]{2,1,0:T(8,128)(2,1)}), bf16[1,4096,128]{2,1,0:T(8,128)(2,1)}) %all-gather.26.cloned.1.call-update) | async-done | bytes 1048592 | tf_op jit(solution)/shard_map/all_gather | solution.py:53
  191.8 2.1 convolution_convert_fusion.3
  193.8 34.4 %all_gather.53 = bf16[2048,128]{1,0:T(8,128)(2,1)S(1)} all-gather(bf16[128,128]{1,0:T(8,128)(2,1)S(1)} %convolution_convert_fusion.3), channel_id=1, replica_groups=mesh['section'=4,'ctx'=16,'tp'=4] {'ctx'}, dimensions={0}, use_global_device_ids=true | all-gather | bytes 557056 | tf_op jit(solution)/shard_map/all_gather | solution.py:96
  228.2 104.3 %all-gather.24.cloned.1.call-done = bf16[1,4096,1024]{2,1,0:T(8,128)(2,1)} async-done(((bf16[1,256,1024]{2,1,0:T(8,128)(2,1)}), bf16[1,4096,1024]{2,1,0:T(8,128)(2,1)}) %all-gather.24.cloned.1.call-update) | async-done | bytes 8388624 | tf_op jit(solution)/shard_map/all_gather | solution.py:51
  332.5 5.0 fusion.76
  339.6 1.7 fusion.28
  341.3 1.7 fusion.108
  343.0 123.9 %all-gather.28.cloned.1.call-done = bf16[1,4096,1024]{2,1,0:T(8,128)(2,1)} async-done(((bf16[1,256,1024]{2,1,0:T(8,128)(2,1)}), bf16[1,4096,1024]{2,1,0:T(8,128)(2,1)}) %all-gather.28.cloned.1.call-update) | async-done | bytes 8388624 | tf_op jit(solution)/shard_map/all_gather | solution.py:54
  466.9 7.2 fusion.36
  474.3 21.0 %reduce-scatter.5.cloned.1.call-done = bf16[128,1024]{1,0:T(8,128)(2,1)} async-done(((bf16[128,4096]{1,0:T(8,128)(2,1)}), bf16[128,1024]{1,0:T(8,128)(2,1)}) %reduce-scatter.5.cloned.1.call-update) | async-done | bytes 262160 | tf_op jit(solution)/shard_map/reduce_scatter | solution.py:122
  496.3 3.1 collective-permute-start
  499.4 5.5 collective-permute-done
  506.9 25.8 %all-gather.14.cloned.1.call-done = bf16[128,4096]{1,0:T(8,128)(2,1)} async-done(((bf16[128,1024]{1,0:T(8,128)(2,1)}), bf16[128,4096]{1,0:T(8,128)(2,1)}) %all-gather.14.cloned.1.call-update) | async-done | bytes 1048592 | tf_op jit(solution)/shard_map/all_gather | solution.py:69
  534.3 2.2 convolution_bitcast_fusion.2
  536.7 7.1 fusion.24
  544.1 37.0 %all_gather.56 = bf16[2048,128]{0,1:T(8,128)(2,1)S(1)} all-gather(bf16[128,128]{0,1:T(8,128)(2,1)S(1)} %pad_maximum_fusion.1), channel_id=1, replica_groups=mesh['section'=4,'ctx'=16,'tp'=4] {'ctx'}, dimensions={0}, use_global_device_ids=true | all-gather | bytes 557056 | tf_op jit(solution)/shard_map/all_gather | solution.py:95
  581.1 1.7 convolution_convert_fusion.2
  582.8 32.2 %all_gather.57 = bf16[2048,128]{1,0:T(8,128)(2,1)S(1)} all-gather(bf16[128,128]{1,0:T(8,128)(2,1)S(1)} %convolution_convert_fusion.2), channel_id=1, replica_groups=mesh['section'=4,'ctx'=16,'tp'=4] {'ctx'}, dimensions={0}, use_global_device_ids=true | all-gather | bytes 557056 | tf_op jit(solution)/shard_map/all_gather | solution.py:96
  617.0 1.7 fusion.30
  618.7 1.7 fusion.102
  621.0 3.9 fusion.39
  625.0 34.8 %reduce-scatter.7.cloned.1.call-done = bf16[128,1024]{1,0:T(8,128)(2,1)} async-done(((bf16[128,4096]{1,0:T(8,128)(2,1)}), bf16[128,1024]{1,0:T(8,128)(2,1)}) %reduce-scatter.7.cloned.1.call-update) | async-done | bytes 262160 | tf_op jit(solution)/shard_map/reduce_scatter | solution.py:122
  660.8 3.1 collective-permute-start.1
  663.9 5.5 collective-permute-done.1
  671.2 26.0 %all-gather.16.cloned.1.call-done = bf16[128,4096]{1,0:T(8,128)(2,1)} async-done(((bf16[128,1024]{1,0:T(8,128)(2,1)}), bf16[128,4096]{1,0:T(8,128)(2,1)}) %all-gather.16.cloned.1.call-update) | async-done | bytes 1048592 | tf_op jit(solution)/shard_map/all_gather | solution.py:69
  698.8 1.8 convolution_bitcast_fusion.1
  700.9 7.1 fusion.22
  708.3 37.4 %all_gather.59 = bf16[2048,128]{0,1:T(8,128)(2,1)S(1)} all-gather(bf16[128,128]{0,1:T(8,128)(2,1)S(1)} %pad_maximum_fusion.2), channel_id=1, replica_groups=mesh['section'=4,'ctx'=16,'tp'=4] {'ctx'}, dimensions={0}, use_global_device_ids=true | all-gather | bytes 557056 | tf_op jit(solution)/shard_map/all_gather | solution.py:95
  745.7 1.7 convolution_convert_fusion.1
  747.5 34.1 %all_gather.60 = bf16[2048,128]{1,0:T(8,128)(2,1)} all-gather(bf16[128,128]{1,0:T(8,128)(2,1)S(1)} %convolution_convert_fusion.1), channel_id=1, replica_groups=mesh['section'=4,'ctx'=16,'tp'=4] {'ctx'}, dimensions={0}, use_global_device_ids=true | all-gather | bytes 557056 | tf_op jit(solution)/shard_map/all_gather | solution.py:96
  783.5 1.7 fusion.32
  787.5 3.9 fusion.42
  791.5 35.3 %reduce-scatter.9.cloned.1.call-done = bf16[128,1024]{1,0:T(8,128)(2,1)} async-done(((bf16[128,4096]{1,0:T(8,128)(2,1)}), bf16[128,1024]{1,0:T(8,128)(2,1)}) %reduce-scatter.9.cloned.1.call-update) | async-done | bytes 262160 | tf_op jit(solution)/shard_map/reduce_scatter | solution.py:122
  827.8 3.1 collective-permute-start.2
  830.9 5.5 collective-permute-done.2
  838.2 26.0 %all-gather.18.cloned.1.call-done = bf16[128,4096]{1,0:T(8,128)(2,1)} async-done(((bf16[128,1024]{1,0:T(8,128)(2,1)}), bf16[128,4096]{1,0:T(8,128)(2,1)}) %all-gather.18.cloned.1.call-update) | async-done | bytes 1048592 | tf_op jit(solution)/shard_map/all_gather | solution.py:69
  865.8 2.2 convolution_bitcast_fusion
  868.2 7.1 fusion.20
  875.6 37.0 %all_gather.62 = bf16[2048,128]{0,1:T(8,128)(2,1)S(1)} all-gather(bf16[128,128]{0,1:T(8,128)(2,1)S(1)} %pad_maximum_fusion.3), channel_id=1, replica_groups=mesh['section'=4,'ctx'=16,'tp'=4] {'ctx'}, dimensions={0}, use_global_device_ids=true | all-gather | bytes 557056 | tf_op jit(solution)/shard_map/all_gather | solution.py:95
  912.6 1.7 convolution_convert_fusion
  914.4 34.2 %all_gather.63 = bf16[2048,128]{1,0:T(8,128)(2,1)} all-gather(bf16[128,128]{1,0:T(8,128)(2,1)S(1)} %convolution_convert_fusion), channel_id=1, replica_groups=mesh['section'=4,'ctx'=16,'tp'=4] {'ctx'}, dimensions={0}, use_global_device_ids=true | all-gather | bytes 557056 | tf_op jit(solution)/shard_map/all_gather | solution.py:96
  950.5 1.7 fusion.34
  954.6 3.9 fusion.45
  958.5 35.3 %reduce-scatter.11.cloned.1.call-done = bf16[128,1024]{1,0:T(8,128)(2,1)} async-done(((bf16[128,4096]{1,0:T(8,128)(2,1)}), bf16[128,1024]{1,0:T(8,128)(2,1)}) %reduce-scatter.11.cloned.1.call-update) | async-done | bytes 262160 | tf_op jit(solution)/shard_map/reduce_scatter | solution.py:122
  (133 shorter events, 37.0 us)
Async XLA Ops:
  6.5 326.0 %copy-start.9 = (f32[1,4096]{1,0:T(1,128)S(1)}, f32[1,4096]{1,0:T(1,128)}, u32[]{:S(2)}) copy-start(f32[1,4096]{1,0:T(1,128)} %param.11) | copy-start | bytes 49156
  6.5 30.0 %all-gather.20.cloned.1.call-start = ((), (), s32[]{:S(2)}) async-start(), calls=%async_computation.11 | async-start | bytes 1310720 | tf_op jit(solution)/shard_map/all_gather | solution.py:69
  7.3 106.7 %all-gather.22.cloned.1.call-start = ((), (), s32[]{:S(2)}) async-start(), calls=%async_computation.12 | async-start | bytes 1114112 | tf_op jit(solution)/shard_map/all_gather | solution.py:52
  8.0 183.8 %all-gather.26.cloned.1.call-start = ((), (), s32[]{:S(2)}) async-start(), calls=%async_computation.14 | async-start | bytes 1114112 | tf_op jit(solution)/shard_map/all_gather | solution.py:53
  8.7 323.8 %all-gather.24.cloned.1.call-start = ((), (), s32[]{:S(2)}) async-start(), calls=%async_computation.13 | async-start | bytes 8912896 | tf_op jit(solution)/shard_map/all_gather | solution.py:51
  9.3 457.6 %all-gather.28.cloned.1.call-start = ((), (), s32[]{:S(2)}) async-start(), calls=%async_computation.15 | async-start | bytes 8912896 | tf_op jit(solution)/shard_map/all_gather | solution.py:54
  9.9 485.3 %reduce-scatter.5.cloned.1.call-start = ((), (), s32[]{:S(2)}) async-start(), calls=%async_computation.4 | async-start | bytes 1310720 | tf_op jit(solution)/shard_map/reduce_scatter | solution.py:122
  10.0 526.5 %copy-start.13 = (f32[64]{0:T(128)}, f32[64]{0:T(128)S(1)}, u32[]{:S(2)}) copy-start(f32[64]{0:T(128)S(1)} %multiply_power_fusion) | copy-start | bytes 772
  11.5 524.9 %copy-start.10 = (f32[128]{0:T(128)}, f32[128]{0:T(128)S(1)}, u32[]{:S(2)}) copy-start(f32[128]{0:T(128)S(1)} %get-tuple-element.5) | copy-start | bytes 1540
  343.0 152.2 %copy-start.6 = (bf16[1,128,1024]{2,1,0:T(8,128)(2,1)S(1)}, bf16[1,128,1024]{2,1,0:T(8,128)(2,1)}, u32[]{:S(2)}) copy-start(bf16[1,128,1024]{2,1,0:T(8,128)(2,1)} %param.8) | copy-start | bytes 786436
  474.2 58.4 %all-gather.14.cloned.1.call-start = ((), (), s32[]{:S(2)}) async-start(), calls=%async_computation.5 | async-start | bytes 1310720 | tf_op jit(solution)/shard_map/all_gather | solution.py:69
  496.3 8.7 collective-permute-start
  506.7 153.1 %reduce-scatter.7.cloned.1.call-start = ((), (), s32[]{:S(2)}) async-start(), calls=%async_computation.6 | async-start | bytes 1310720 | tf_op jit(solution)/shard_map/reduce_scatter | solution.py:122
  532.7 48.4 %copy-start.1 = (bf16[128,4096]{1,0:T(8,128)(2,1)S(1)}, bf16[128,4096]{1,0:T(8,128)(2,1)}, u32[]{:S(2)}) copy-start(bf16[128,4096]{1,0:T(8,128)(2,1)} %all-gather.14.cloned.1.call-done) | copy-start | bytes 3145732
  617.0 3.5 slice-start
  618.7 2.3 slice-start.1
  620.4 39.4 %copy-start.4 = (bf16[128,1024]{1,0:T(8,128)(2,1)S(1)}, bf16[128,1024]{1,0:T(8,128)(2,1)}, u32[]{:S(2)}) copy-start(bf16[128,1024]{1,0:T(8,128)(2,1)} %bitcast_select_fusion.6) | copy-start | bytes 786436
  620.4 78.4 %copy-start.17 = (bf16[1,4096,128]{2,1,0:T(8,128)(2,1)S(1)}, bf16[1,4096,128]{2,1,0:T(8,128)(2,1)}, u32[]{:S(2)}) copy-start(bf16[1,4096,128]{2,1,0:T(8,128)(2,1)} %all-gather.22.cloned.1.call-done) | copy-start | bytes 3145732
  620.5 80.2 %copy-start.11 = (f32[128]{0:T(128)S(1)}, f32[128]{0:T(128)}, u32[]{:S(2)}) copy-start(f32[128]{0:T(128)} %copy-done.10) | copy-start | bytes 1540
  620.5 80.2 %copy-start.14 = (f32[64]{0:T(128)S(1)}, f32[64]{0:T(128)}, u32[]{:S(2)}) copy-start(f32[64]{0:T(128)} %copy-done.13) | copy-start | bytes 772
  624.9 72.3 %all-gather.16.cloned.1.call-start = ((), (), s32[]{:S(2)}) async-start(), calls=%async_computation.7 | async-start | bytes 1310720 | tf_op jit(solution)/shard_map/all_gather | solution.py:69
  660.8 8.6 collective-permute-start.1
  671.2 155.6 %reduce-scatter.9.cloned.1.call-start = ((), (), s32[]{:S(2)}) async-start(), calls=%async_computation.8 | async-start | bytes 1310720 | tf_op jit(solution)/shard_map/reduce_scatter | solution.py:122
  697.2 48.5 %copy-start.2 = (bf16[128,4096]{1,0:T(8,128)(2,1)S(1)}, bf16[128,4096]{1,0:T(8,128)(2,1)}, u32[]{:S(2)}) copy-start(bf16[128,4096]{1,0:T(8,128)(2,1)} %all-gather.16.cloned.1.call-done) | copy-start | bytes 3145732
  781.9 3.3 copy-start.8
  783.5 3.5 slice-start.2
  785.2 2.3 slice-start.3
  786.9 39.8 %copy-start.5 = (bf16[128,1024]{1,0:T(8,128)(2,1)S(1)}, bf16[128,1024]{1,0:T(8,128)(2,1)}, u32[]{:S(2)}) copy-start(bf16[128,1024]{1,0:T(8,128)(2,1)} %bitcast_select_fusion.5) | copy-start | bytes 786436
  786.9 81.0 %copy-start.12 = (f32[128]{0:T(128)S(1)}, f32[128]{0:T(128)}, u32[]{:S(2)}) copy-start(f32[128]{0:T(128)} %copy-done.10) | copy-start | bytes 1540
  786.9 81.0 %copy-start.15 = (f32[64]{0:T(128)S(1)}, f32[64]{0:T(128)}, u32[]{:S(2)}) copy-start(f32[64]{0:T(128)} %copy-done.13) | copy-start | bytes 772
  791.4 72.8 %all-gather.18.cloned.1.call-start = ((), (), s32[]{:S(2)}) async-start(), calls=%async_computation.9 | async-start | bytes 1310720 | tf_op jit(solution)/shard_map/all_gather | solution.py:69
  827.8 8.7 collective-permute-start.2
  838.1 155.6 %reduce-scatter.11.cloned.1.call-start = ((), (), s32[]{:S(2)}) async-start(), calls=%async_computation.10 | async-start | bytes 1310720 | tf_op jit(solution)/shard_map/reduce_scatter | solution.py:122
  864.2 48.4 %copy-start = (bf16[128,4096]{1,0:T(8,128)(2,1)S(1)}, bf16[128,4096]{1,0:T(8,128)(2,1)}, u32[]{:S(2)}) copy-start(bf16[128,4096]{1,0:T(8,128)(2,1)} %all-gather.18.cloned.1.call-done) | copy-start | bytes 3145732
  865.8 9.5 copy-start.16
  949.0 3.3 copy-start.7
  950.5 3.5 slice-start.4
  952.3 2.3 slice-start.5
  954.0 39.8 %copy-start.3 = (bf16[128,1024]{1,0:T(8,128)(2,1)S(1)}, bf16[128,1024]{1,0:T(8,128)(2,1)}, u32[]{:S(2)}) copy-start(bf16[128,1024]{1,0:T(8,128)(2,1)} %bitcast_select_fusion.4) | copy-start | bytes 786436
Sparse Core Ops, SparseCore 0:
  9.1 27.3 all-gather.19
  39.1 74.7 all-gather.21
  116.6 75.1 all-gather.25
  194.2 138.2 all-gather.23
  334.9 131.9 all-gather.27
  474.3 20.8 reduce-scatter.4
  506.8 25.8 all-gather.13
  625.1 34.6 reduce-scatter.6
  671.3 25.8 all-gather.15
  791.5 35.1 reduce-scatter.8
  838.3 25.8 all-gather.17
  958.6 35.1 reduce-scatter.10
where the time goes:
time: 1010 us; the launch traced here: 1000 us
  waiting for transfers between devices  595 us (59%)
  blocking collectives  280 us (28%)
  matrix products  73.8 us (7%)
  other arithmetic  27.1 us (3%)
  between operations  14.5 us (1%)
    all_gather x4, blocking collectives, on_device(): key_piece = lax.all_gather(key_vecs, 'ctx', axis=0, tiled=True)  145 us
    all_gather x4, blocking collectives, on_device(): value_piece = lax.all_gather(values, 'ctx', axis=0, tiled=True)  135 us
    reduce_scatter x4, waiting for transfers between devices, on_device(): lax.psum_scatter(lax.dot_general(attended, output_weights, (((1,), (1,)),...  126 us
    all_gather x1, waiting for transfers between devices, on_device(): lax.all_gather(w_out[0], 'ctx', axis=0, tiled=True)  124 us
    all_gather x1, waiting for transfers between devices, on_device(): lax.all_gather(w_query[0], 'ctx', axis=0, tiled=True)  104 us
    all_gather x4, waiting for transfers between devices, on_device(): full_rows = lax.all_gather(current, 'tp', axis=1, tiled=True)  102 us
    all_gather x1, waiting for transfers between devices, on_device(): lax.all_gather(w_key[0], 'ctx', axis=0, tiled=True)  75.9 us
    all_gather x1, waiting for transfers between devices, on_device(): lax.all_gather(w_value[0], 'ctx', axis=0, tiled=True)  42.2 us
  transfers between devices with their start and end apart: 15, of which 15 were waited for; matrix products, arithmetic and copies ran while one was open for 2% of the time, Pallas kernels for 0%

commit v1 on v0

--- a/solution.py
+++ b/solution.py
@@ -8,6 +8,11 @@
 EPS = 1e-05
 ROPE_BASE = 500000.0
 NEGATIVE = -1e30
+
+
+def all_by_exchange(x, mesh_axis, dim):
+    sent = jnp.stack([x] * lax.axis_size(mesh_axis))
+    return jnp.concatenate(lax.all_to_all(sent, mesh_axis, 0, 0), axis=dim)
 
 
 def shifted(x, axis, by):
@@ -48,7 +53,7 @@
     row_count = hidden_in.shape[1]
     sections = lax.axis_size("section")
     query_weights, key_weights, value_weights, output_weights = (
-        lax.all_gather(w_query[0], "ctx", axis=0, tiled=True),
+        all_by_exchange(w_query[0], "ctx", 0),
         lax.all_gather(w_key[0], "ctx", axis=0, tiled=True),
         lax.all_gather(w_value[0], "ctx", axis=0, tiled=True),
         lax.all_gather(w_out[0], "ctx", axis=0, tiled=True),

time: 1010 us -> 942 us (0.933)
  waiting for transfers between devices: 595 us -> 476 us
  local copies, waits for them, and re-layouts: 3.35 us -> 31.2 us
  blocking collectives: 280 us -> 307 us
  starting transfers between devices: 9.98 us -> 22.4 us
  matrix products: 73.8 us -> 63.5 us
    all_gather x1 -> x0, waiting for transfers between devices: 104 us -> none  [on_device(): lax.all_gather(w_query[0], 'ctx', axis=0, tiled=True)]
    all_gather x1, waiting for transfers between devices: 75.9 us -> 135 us  [on_device(): lax.all_gather(w_key[0], 'ctx', axis=0, tiled=True)]
    all_gather x1, waiting for transfers between devices: 124 us -> 68.7 us  [on_device(): lax.all_gather(w_out[0], 'ctx', axis=0, tiled=True)]
    all_gather x4, blocking collectives: 145 us -> 176 us  [on_device(): key_piece = lax.all_gather(key_vecs, 'ctx', axis=0, tiled=True)]
    all_to_all x0 -> x1, local copies, waits for them, and re-layouts: none -> 12.3 us  [all_by_exchange(): return jnp.concatenate(lax.all_to_all(sent, mesh_axis, 0, 0), axis=dim)]
    all_to_all x0 -> x1, starting transfers between devices: none -> 11.8 us  [all_by_exchange(): return jnp.concatenate(lax.all_to_all(sent, mesh_axis, 0, 0), axis=dim)]
    dot_general x0 -> x1, local copies, waits for them, and re-layouts: none -> 11.7 us  [on_device(): jnp.dot(normed, query_weights, preferred_element_type=jnp.float32)]
  transfers between devices with their start and end apart: 15 -> 15, of which waited for: 15 -> 14; matrix products, arithmetic and copies ran while one was open for 2% -> 5% of each run, Pallas kernels for 0% -> 0%
where the time goes in v1:
time: 942 us; the launch traced here: 937 us
  waiting for transfers between devices  476 us (51%)
  blocking collectives  307 us (33%)
  matrix products  63.5 us (7%)
  local copies, waits for them, and re-layouts  31.2 us (3%)
  other arithmetic  22.5 us (2%)
  starting transfers between devices  22.4 us (2%)
  between operations  14 us (1%)
    all_gather x4, blocking collectives, on_device(): key_piece = lax.all_gather(key_vecs, 'ctx', axis=0, tiled=True)  176 us
    all_gather x1, waiting for transfers between devices, on_device(): lax.all_gather(w_key[0], 'ctx', axis=0, tiled=True)  135 us
    all_gather x4, blocking collectives, on_device(): value_piece = lax.all_gather(values, 'ctx', axis=0, tiled=True)  131 us
    reduce_scatter x4, waiting for transfers between devices, on_device(): lax.psum_scatter(lax.dot_general(attended, output_weights, (((1,), (1,)),...  126 us
    all_gather x4, waiting for transfers between devices, on_device(): full_rows = lax.all_gather(current, 'tp', axis=1, tiled=True)  95.1 us
    all_gather x1, waiting for transfers between devices, on_device(): lax.all_gather(w_out[0], 'ctx', axis=0, tiled=True)  68.7 us
    all_gather x1, waiting for transfers between devices, on_device(): lax.all_gather(w_value[0], 'ctx', axis=0, tiled=True)  32.7 us
    dot_general x4, matrix products, on_device(): jnp.dot(normed, query_weights, preferred_element_type=jnp.float32)  24.7 us
  transfers between devices with their start and end apart: 15, of which 14 were waited for; matrix products, arithmetic and copies ran while one was open for 5% of the time, Pallas kernels for 0%

profile of v1, /device:TPU:1, one launch (start us, length us, event | category | flops | bytes accessed | tf_op | source)
XLA Modules:
  0.0 937.0 jit_solution(6654825240659565576)
XLA Ops:
  9.3 4.1 stack.18
  13.3 11.8 %all-to-all-start = ((bf16[16,256,1024]{1,2,0:T(8,128)(2,1)}), bf16[16,256,1024]{1,2,0:T(8,128)(2,1)}, u32[]{:S(2)}, u32[]{:S(2)}) async-start(bf16[16,256,1024]{1,2,0:T(8,128)(2,1)} %stack.18), calls=%async_computation | async-start | bytes 16777216 | tf_op jit(solution)/shard_map/all_to_all | solution.py:15
  27.3 18.0 %all-gather.18.cloned.1.call-done = bf16[1,128,4096]{2,1,0:T(8,128)(2,1)} async-done(((bf16[1,128,1024]{2,1,0:T(8,128)(2,1)}), bf16[1,128,4096]{2,1,0:T(8,128)(2,1)}) %all-gather.18.cloned.1.call-update) | async-done | bytes 1048592 | tf_op jit(solution)/shard_map/all_gather | solution.py:74
  46.9 134.5 %all-gather.20.cloned.1.call-done = bf16[1,4096,128]{2,1,0:T(8,128)(2,1)} async-done(((bf16[1,256,128]{2,1,0:T(8,128)(2,1)}), bf16[1,4096,128]{2,1,0:T(8,128)(2,1)}) %all-gather.20.cloned.1.call-update) | async-done | bytes 1048592 | tf_op jit(solution)/shard_map/all_gather | solution.py:57
  181.4 2.2 convolution_bitcast_fusion.3
  183.8 65.1 %all_gather.47 = bf16[2048,128]{0,1:T(8,128)(2,1)S(1)} all-gather(bf16[128,128]{0,1:T(8,128)(2,1)S(1)} %pad_maximum_fusion), channel_id=1, replica_groups=mesh['section'=4,'ctx'=16,'tp'=4] {'ctx'}, dimensions={0}, use_global_device_ids=true | all-gather | bytes 557056 | tf_op jit(solution)/shard_map/all_gather | solution.py:100
  248.9 32.7 %all-gather.22.cloned.1.call-done = bf16[1,4096,128]{2,1,0:T(8,128)(2,1)} async-done(((bf16[1,256,128]{2,1,0:T(8,128)(2,1)}), bf16[1,4096,128]{2,1,0:T(8,128)(2,1)}) %all-gather.22.cloned.1.call-update) | async-done | bytes 1048592 | tf_op jit(solution)/shard_map/all_gather | solution.py:58
  281.5 2.0 convolution_convert_fusion.3
  283.6 34.6 %all_gather.49 = bf16[2048,128]{1,0:T(8,128)(2,1)S(1)} all-gather(bf16[128,128]{1,0:T(8,128)(2,1)S(1)} %convolution_convert_fusion.3), channel_id=1, replica_groups=mesh['section'=4,'ctx'=16,'tp'=4] {'ctx'}, dimensions={0}, use_global_device_ids=true | all-gather | bytes 557056 | tf_op jit(solution)/shard_map/all_gather | solution.py:101
  318.2 12.3 %copy.58 = bf16[16,256,1024]{2,1,0:T(8,128)(2,1)} copy(bf16[16,256,1024]{1,2,0:T(8,128)(2,1)} %all-to-all-done) | data formatting | bytes 16777216 | tf_op jit(solution)/shard_map/all_to_all | solution.py:15
  330.5 11.7 %copy.59 = bf16[1024,4096]{1,0:T(8,128)(2,1)} copy(bf16[1024,4096]{0,1:T(8,128)(2,1)} %bitcast.290) | data formatting | bytes 16777216 | tf_op jit(solution)/shard_map/dot_general | solution.py:81
  342.3 6.2 fusion.78
  349.9 1.7 fusion.20
  351.7 1.7 fusion.105
  353.4 68.7 %all-gather.24.cloned.1.call-done = bf16[1,4096,1024]{2,1,0:T(8,128)(2,1)} async-done(((bf16[1,256,1024]{2,1,0:T(8,128)(2,1)}), bf16[1,4096,1024]{2,1,0:T(8,128)(2,1)}) %all-gather.24.cloned.1.call-update) | async-done | bytes 8388624 | tf_op jit(solution)/shard_map/all_gather | solution.py:59
  422.1 7.2 fusion.28
  429.5 21.0 %reduce-scatter.5.cloned.1.call-done = bf16[128,1024]{1,0:T(8,128)(2,1)} async-done(((bf16[128,4096]{1,0:T(8,128)(2,1)}), bf16[128,1024]{1,0:T(8,128)(2,1)}) %reduce-scatter.5.cloned.1.call-update) | async-done | bytes 262160 | tf_op jit(solution)/shard_map/reduce_scatter | solution.py:127
  451.5 3.1 collective-permute-start
  454.6 5.5 collective-permute-done
  461.5 25.4 %all-gather.12.cloned.1.call-done = bf16[128,4096]{1,0:T(8,128)(2,1)} async-done(((bf16[128,1024]{1,0:T(8,128)(2,1)}), bf16[128,4096]{1,0:T(8,128)(2,1)}) %all-gather.12.cloned.1.call-update) | async-done | bytes 1048592 | tf_op jit(solution)/shard_map/all_gather | solution.py:74
  488.5 6.2 fusion.72
  495.7 37.0 %all_gather.52 = bf16[2048,128]{0,1:T(8,128)(2,1)S(1)} all-gather(bf16[128,128]{0,1:T(8,128)(2,1)S(1)} %pad_maximum_fusion.1), channel_id=1, replica_groups=mesh['section'=4,'ctx'=16,'tp'=4] {'ctx'}, dimensions={0}, use_global_device_ids=true | all-gather | bytes 557056 | tf_op jit(solution)/shard_map/all_gather | solution.py:100
  533.3 32.2 %all_gather.53 = bf16[2048,128]{1,0:T(8,128)(2,1)S(1)} all-gather(bf16[128,128]{1,0:T(8,128)(2,1)S(1)} %convolution_convert_fusion.2), channel_id=1, replica_groups=mesh['section'=4,'ctx'=16,'tp'=4] {'ctx'}, dimensions={0}, use_global_device_ids=true | all-gather | bytes 557056 | tf_op jit(solution)/shard_map/all_gather | solution.py:101
  566.9 1.7 fusion.22
  568.6 1.7 fusion.99
  570.9 3.8 fusion.31
  574.8 34.9 %reduce-scatter.7.cloned.1.call-done = bf16[128,1024]{1,0:T(8,128)(2,1)} async-done(((bf16[128,4096]{1,0:T(8,128)(2,1)}), bf16[128,1024]{1,0:T(8,128)(2,1)}) %reduce-scatter.7.cloned.1.call-update) | async-done | bytes 262160 | tf_op jit(solution)/shard_map/reduce_scatter | solution.py:127
  610.8 3.1 collective-permute-start.1
  613.9 5.5 collective-permute-done.1
  620.4 25.9 %all-gather.14.cloned.1.call-done = bf16[128,4096]{1,0:T(8,128)(2,1)} async-done(((bf16[128,1024]{1,0:T(8,128)(2,1)}), bf16[128,4096]{1,0:T(8,128)(2,1)}) %all-gather.14.cloned.1.call-update) | async-done | bytes 1048592 | tf_op jit(solution)/shard_map/all_gather | solution.py:74
  647.9 6.2 fusion.70
  655.0 37.0 %all_gather.55 = bf16[2048,128]{0,1:T(8,128)(2,1)S(1)} all-gather(bf16[128,128]{0,1:T(8,128)(2,1)S(1)} %pad_maximum_fusion.2), channel_id=1, replica_groups=mesh['section'=4,'ctx'=16,'tp'=4] {'ctx'}, dimensions={0}, use_global_device_ids=true | all-gather | bytes 557056 | tf_op jit(solution)/shard_map/all_gather | solution.py:100
  692.6 32.1 %all_gather.56 = bf16[2048,128]{1,0:T(8,128)(2,1)S(1)} all-gather(bf16[128,128]{1,0:T(8,128)(2,1)S(1)} %convolution_convert_fusion.1), channel_id=1, replica_groups=mesh['section'=4,'ctx'=16,'tp'=4] {'ctx'}, dimensions={0}, use_global_device_ids=true | all-gather | bytes 557056 | tf_op jit(solution)/shard_map/all_gather | solution.py:101
  726.1 1.7 fusion.24
  727.8 1.7 fusion.93
  730.1 3.8 fusion.34
  734.0 34.9 %reduce-scatter.9.cloned.1.call-done = bf16[128,1024]{1,0:T(8,128)(2,1)} async-done(((bf16[128,4096]{1,0:T(8,128)(2,1)}), bf16[128,1024]{1,0:T(8,128)(2,1)}) %reduce-scatter.9.cloned.1.call-update) | async-done | bytes 262160 | tf_op jit(solution)/shard_map/reduce_scatter | solution.py:127
  769.9 3.1 collective-permute-start.2
  773.1 5.5 collective-permute-done.2
  779.6 25.8 %all-gather.16.cloned.1.call-done = bf16[128,4096]{1,0:T(8,128)(2,1)} async-done(((bf16[128,1024]{1,0:T(8,128)(2,1)}), bf16[128,4096]{1,0:T(8,128)(2,1)}) %all-gather.16.cloned.1.call-update) | async-done | bytes 1048592 | tf_op jit(solution)/shard_map/all_gather | solution.py:74
  805.4 1.6 fusion.62
  807.0 6.2 fusion.68
  814.1 37.0 %all_gather.58 = bf16[2048,128]{0,1:T(8,128)(2,1)S(1)} all-gather(bf16[128,128]{0,1:T(8,128)(2,1)S(1)} %pad_maximum_fusion.3), channel_id=1, replica_groups=mesh['section'=4,'ctx'=16,'tp'=4] {'ctx'}, dimensions={0}, use_global_device_ids=true | all-gather | bytes 557056 | tf_op jit(solution)/shard_map/all_gather | solution.py:100
  851.7 32.2 %all_gather.59 = bf16[2048,128]{1,0:T(8,128)(2,1)S(1)} all-gather(bf16[128,128]{1,0:T(8,128)(2,1)S(1)} %convolution_convert_fusion), channel_id=1, replica_groups=mesh['section'=4,'ctx'=16,'tp'=4] {'ctx'}, dimensions={0}, use_global_device_ids=true | all-gather | bytes 557056 | tf_op jit(solution)/shard_map/all_gather | solution.py:101
  885.4 1.7 fusion.26
  887.1 1.7 fusion.87
  889.4 3.8 fusion.37
  893.2 34.9 %reduce-scatter.11.cloned.1.call-done = bf16[128,1024]{1,0:T(8,128)(2,1)} async-done(((bf16[128,4096]{1,0:T(8,128)(2,1)}), bf16[128,1024]{1,0:T(8,128)(2,1)}) %reduce-scatter.11.cloned.1.call-update) | async-done | bytes 262160 | tf_op jit(solution)/shard_map/reduce_scatter | solution.py:127
  (119 shorter events, 30.2 us)
Async XLA Ops:
  6.5 38.8 %all-gather.18.cloned.1.call-start = ((), (), s32[]{:S(2)}) async-start(), calls=%async_computation.12 | async-start | bytes 1310720 | tf_op jit(solution)/shard_map/all_gather | solution.py:74
  7.3 174.1 %all-gather.20.cloned.1.call-start = ((), (), s32[]{:S(2)}) async-start(), calls=%async_computation.13 | async-start | bytes 1114112 | tf_op jit(solution)/shard_map/all_gather | solution.py:57
  13.3 13.2 %copy-start.10 = (s32[32]{0:T(128)S(1)}, s32[32]{0:T(128)}, u32[]{:S(2)}) copy-start(s32[32]{0:T(128)} %param.10) | copy-start | bytes 388
  13.3 168.1 %copy-start.9 = (f32[1,4096]{1,0:T(1,128)S(1)}, f32[1,4096]{1,0:T(1,128)}, u32[]{:S(2)}) copy-start(f32[1,4096]{1,0:T(1,128)} %param.11) | copy-start | bytes 49156
  13.3 304.9 %all-to-all-start = ((bf16[16,256,1024]{1,2,0:T(8,128)(2,1)}), bf16[16,256,1024]{1,2,0:T(8,128)(2,1)}, u32[]{:S(2)}, u32[]{:S(2)}) async-start(bf16[16,256,1024]{1,2,0:T(8,128)(2,1)} %stack.18), calls=%async_computation | async-start | bytes 16777216 | tf_op jit(solution)/shard_map/all_to_all | solution.py:15
  25.1 256.4 %all-gather.22.cloned.1.call-start = ((), (), s32[]{:S(2)}) async-start(), calls=%async_computation.14 | async-start | bytes 1114112 | tf_op jit(solution)/shard_map/all_gather | solution.py:58
  25.8 396.3 %all-gather.24.cloned.1.call-start = ((), (), s32[]{:S(2)}) async-start(), calls=%async_computation.15 | async-start | bytes 8912896 | tf_op jit(solution)/shard_map/all_gather | solution.py:59
  26.4 424.0 %reduce-scatter.5.cloned.1.call-start = ((), (), s32[]{:S(2)}) async-start(), calls=%async_computation.5 | async-start | bytes 1310720 | tf_op jit(solution)/shard_map/reduce_scatter | solution.py:127
  330.5 11.7 %copy-start = (bf16[1,128,4096]{2,1,0:T(8,128)(2,1)S(1)}, bf16[1,128,4096]{2,1,0:T(8,128)(2,1)}, u32[]{:S(2)}) copy-start(bf16[1,128,4096]{2,1,0:T(8,128)(2,1)} %all-gather.18.cloned.1.call-done) | copy-start | bytes 3145732
  353.4 97.1 %copy-start.7 = (bf16[1,128,1024]{2,1,0:T(8,128)(2,1)S(1)}, bf16[1,128,1024]{2,1,0:T(8,128)(2,1)}, u32[]{:S(2)}) copy-start(bf16[1,128,1024]{2,1,0:T(8,128)(2,1)} %param.8) | copy-start | bytes 786436
  353.4 106.8 %copy-start.8 = (bf16[3,128,1024]{2,1,0:T(8,128)(2,1)S(1)}, bf16[3,128,1024]{2,1,0:T(8,128)(2,1)}, u32[]{:S(2)}) copy-start(bf16[3,128,1024]{2,1,0:T(8,128)(2,1)} %param.9) | copy-start | bytes 2359300
  429.4 65.4 %copy-start.11 = (bf16[1,4096,128]{2,1,0:T(8,128)(2,1)S(1)}, bf16[1,4096,128]{2,1,0:T(8,128)(2,1)}, u32[]{:S(2)}) copy-start(bf16[1,4096,128]{2,1,0:T(8,128)(2,1)} %all-gather.20.cloned.1.call-done) | copy-start | bytes 3145732
  429.4 57.5 %all-gather.12.cloned.1.call-start = ((), (), s32[]{:S(2)}) async-start(), calls=%async_computation.6 | async-start | bytes 1310720 | tf_op jit(solution)/shard_map/all_gather | solution.py:74
  451.5 8.7 collective-permute-start
  460.9 148.8 %reduce-scatter.7.cloned.1.call-start = ((), (), s32[]{:S(2)}) async-start(), calls=%async_computation.7 | async-start | bytes 1310720 | tf_op jit(solution)/shard_map/reduce_scatter | solution.py:127
  486.9 7.9 copy-start.2
  488.5 44.2 %copy-start.12 = (bf16[1,4096,128]{2,1,0:T(8,128)(2,1)S(1)}, bf16[1,4096,128]{2,1,0:T(8,128)(2,1)}, u32[]{:S(2)}) copy-start(bf16[1,4096,128]{2,1,0:T(8,128)(2,1)} %all-gather.22.cloned.1.call-done) | copy-start | bytes 3145732
  566.9 3.4 slice-start
  568.6 2.3 slice-start.1
  570.3 39.4 %copy-start.5 = (bf16[128,1024]{1,0:T(8,128)(2,1)S(1)}, bf16[128,1024]{1,0:T(8,128)(2,1)}, u32[]{:S(2)}) copy-start(bf16[128,1024]{1,0:T(8,128)(2,1)} %bitcast_select_fusion.6) | copy-start | bytes 786436
  574.8 71.5 %all-gather.14.cloned.1.call-start = ((), (), s32[]{:S(2)}) async-start(), calls=%async_computation.8 | async-start | bytes 1310720 | tf_op jit(solution)/shard_map/all_gather | solution.py:74
  610.8 8.6 collective-permute-start.1
  620.2 148.8 %reduce-scatter.9.cloned.1.call-start = ((), (), s32[]{:S(2)}) async-start(), calls=%async_computation.9 | async-start | bytes 1310720 | tf_op jit(solution)/shard_map/reduce_scatter | solution.py:127
  646.3 7.9 copy-start.3
  647.9 44.2 %copy-start.13 = (bf16[1,4096,128]{2,1,0:T(8,128)(2,1)S(1)}, bf16[1,4096,128]{2,1,0:T(8,128)(2,1)}, u32[]{:S(2)}) copy-start(bf16[1,4096,128]{2,1,0:T(8,128)(2,1)} %all-gather.22.cloned.1.call-done) | copy-start | bytes 3145732
  726.1 3.4 slice-start.2
  727.8 2.3 slice-start.3
  729.6 39.4 %copy-start.6 = (bf16[128,1024]{1,0:T(8,128)(2,1)S(1)}, bf16[128,1024]{1,0:T(8,128)(2,1)}, u32[]{:S(2)}) copy-start(bf16[128,1024]{1,0:T(8,128)(2,1)} %bitcast_select_fusion.5) | copy-start | bytes 786436
  734.0 71.4 %all-gather.16.cloned.1.call-start = ((), (), s32[]{:S(2)}) async-start(), calls=%async_computation.10 | async-start | bytes 1310720 | tf_op jit(solution)/shard_map/all_gather | solution.py:74
  769.9 8.7 collective-permute-start.2
  779.3 148.8 %reduce-scatter.11.cloned.1.call-start = ((), (), s32[]{:S(2)}) async-start(), calls=%async_computation.11 | async-start | bytes 1310720 | tf_op jit(solution)/shard_map/reduce_scatter | solution.py:127
  805.4 7.9 copy-start.1
  807.0 44.2 %copy-start.14 = (bf16[1,4096,128]{2,1,0:T(8,128)(2,1)S(1)}, bf16[1,4096,128]{2,1,0:T(8,128)(2,1)}, u32[]{:S(2)}) copy-start(bf16[1,4096,128]{2,1,0:T(8,128)(2,1)} %all-gather.22.cloned.1.call-done) | copy-start | bytes 3145732
  885.4 3.5 slice-start.4
  887.1 2.3 slice-start.5
  888.8 39.3 %copy-start.4 = (bf16[128,1024]{1,0:T(8,128)(2,1)S(1)}, bf16[128,1024]{1,0:T(8,128)(2,1)}, u32[]{:S(2)}) copy-start(bf16[128,1024]{1,0:T(8,128)(2,1)} %bitcast_select_fusion.4) | copy-start | bytes 786436
Sparse Core Ops, SparseCore 0:
  9.1 36.1 all-gather.17
  47.9 133.4 all-gather.19
  184.0 97.4 all-gather.21
  284.0 138.1 all-gather.23
  429.5 20.8 reduce-scatter.4
  461.0 25.8 all-gather.11
  574.9 34.7 reduce-scatter.6
  620.3 25.9 all-gather.13
  734.1 34.7 reduce-scatter.8
  779.5 25.8 all-gather.15
  893.4 34.6 reduce-scatter.10
